TPU v7x, 256 devices: a whole 4x4x8 slice. The times are simulated.
256 devices in a mesh: table: 16 (over x, y), dp: 8 (over z), col: 2 (over core).
Axes of the slice: x: 4, y: 4, z: 8, core: 2. Of those that a mesh axis runs over, the one named last changes fastest.
Arguments:
- table_weights: float32 [32768, 512], P('table', 'col'), may hold values from -6 to 6
- moment_first: float32 [32768, 512], P('table', 'col'), may hold values from -3 to 3
- moment_second: float32 [32768], P('table'), may hold values from 0.1 to 2
- hot_slices: int32 [16, 2], replicated, may hold values from 0 to 31, as said below
- upstream_grad: bfloat16 [131072, 512], P(('table', 'dp'), 'col'), may hold values from -20 to 20
- dedup_map: int32 [131072, 32], P(('table', 'dp')), may hold values from 0 to 4095, as said below
- unique_rows: int32 [128, 16, 256], P(('table', 'dp')), may hold values from 0 to 32767, as said below
- row_counts: int32 [128, 16], P(('table', 'dp')), may hold values from 192 to 256, as said below
Outputs:
- new_weights: float32 [32768, 512], P('table', 'col')
- new_first: float32 [32768, 512], P('table', 'col')
- new_second: float32 [32768], P('table')
Inputs may be any that keep to these rules, and one draw needn't show every extreme that they name: `hot_slices`: each row holds 2 different slice numbers below 32. `unique_rows`: for source device s and owner t, the first row_counts[s, t] entries are different rows r with physical(r) on table index t; the remaining entries are not used. `row_counts`: in every draw some owner receives 256 used slots from every source device. `dedup_map`: an entry in a row of source device s is a used slot t * 256 + k with k < row_counts[s, t].
All inputs are finite; a program needn't handle non-finite values.
Results may differ from a plain program's by a relative error of at most 0.0003.
Values sent between devices are 32-bit elements; how exact they have to be, the bound alone decides.
No kernel may reach another device: no remote copies, remote signals or barrier semaphores. Data moves between devices by JAX's collectives and lax.ppermute only.
A program may use at most 64 MiB of HBM per device.

v0:
```python
import jax
import jax.numpy as jnp
from jax import lax
from jax.sharding import PartitionSpec as P

SLICE = 64
beta_one = 0.9
beta_two = 0.99
learn_rate = 0.1
eps_value = 1e-08


def partner_2(block, axis, distance):
    count = lax.axis_size(axis)
    route = []
    for low in range(count):
        high = low | 1 << distance
        if high != low and high < count:
            route += [(low, high), (high, low)]
    return lax.ppermute(block, axis, route)


def local_targets(logical_rows, hot_slices, rows_dev):
    n_table = hot_slices.shape[0]
    row_owner = logical_rows // rows_dev
    local_row = logical_rows % rows_dev
    row_piece = local_row // SLICE
    row_offset = local_row % SLICE
    matches = hot_slices[row_owner] == row_piece[..., None]
    partner = (row_owner + n_table // 2) % n_table
    partner_piece = jnp.sum(jnp.where(matches, hot_slices[partner], 0), axis=-1)
    return jnp.where(jnp.any(matches, axis=-1), partner_piece * SLICE + row_offset, local_row)


def adam_rows(weights, first, second, gradient, squares, full_width):
    new_second = beta_two * second + (1.0 - beta_two) * (squares / full_width)
    new_first = beta_one * first + (1.0 - beta_one) * gradient
    scaled = jnp.sqrt(new_second / (1.0 - beta_two**8)) + eps_value
    new_weights = weights - learn_rate * (new_first / (1.0 - beta_one**8)) / scaled[:, None]
    return (new_weights, new_first, new_second)


def on_device(
    table_weights,
    moment_first,
    moment_second,
    hot_slices,
    upstream_grad,
    dedup_map,
    unique_rows,
    row_counts,
):
    n_table = lax.axis_size("table")
    position = lax.axis_index("table")
    rows_dev, col_width = table_weights.shape
    own_hot = hot_slices[position]
    n_hots = own_hot.shape[0]
    starts = [own_hot[k] * SLICE for k in range(n_hots)]
    out_weights = jnp.stack(
        [lax.dynamic_slice_in_dim(table_weights, starts[k], SLICE, 0) for k in range(n_hots)]
    )
    out_first = jnp.stack(
        [lax.dynamic_slice_in_dim(moment_first, starts[k], SLICE, 0) for k in range(n_hots)]
    )
    out_second = jnp.stack(
        [lax.dynamic_slice_in_dim(moment_second, starts[k], SLICE, 0) for k in range(n_hots)]
    )
    swap_bit = n_table.bit_length() - 2
    incoming = partner_2((out_weights, out_first, out_second), "table", swap_bit)
    placed_weights = table_weights
    placed_first = moment_first
    placed_second = moment_second
    for k in range(n_hots):
        placed_weights = lax.dynamic_update_slice_in_dim(
            placed_weights, incoming[0][k], starts[k], 0
        )
        placed_first = lax.dynamic_update_slice_in_dim(placed_first, incoming[1][k], starts[k], 0)
        placed_second = lax.dynamic_update_slice_in_dim(placed_second, incoming[2][k], starts[k], 0)
    slot_cap = unique_rows.shape[2]
    valid = jnp.arange(slot_cap)[None, :] < row_counts[0][:, None]
    targets = jnp.where(valid, local_targets(unique_rows[0], hot_slices, rows_dev), rows_dev)
    slot_iota = jnp.arange(slot_cap)

    def owner_block(carry, owner):
        wanted = slot_iota + owner * slot_cap
        tally = jnp.sum(
            (dedup_map[None, :, :] == wanted[:, None, None]).astype(jnp.float32), axis=2
        )
        block = jnp.dot(
            tally.astype(jnp.bfloat16), upstream_grad, preferred_element_type=jnp.float32
        )
        return (carry, block)

    _, slot_grad = lax.scan(owner_block, 0, jnp.arange(n_table))
    got_grad, got_target = (
        lax.all_to_all(slot_grad, "table", split_axis=0, concat_axis=0, tiled=True),
        lax.all_to_all(targets, "table", split_axis=0, concat_axis=0, tiled=True),
    )
    row_iota = jnp.arange(rows_dev)

    def add_source(total, inputs):
        grad_block, target_block = inputs
        select = (row_iota[:, None] == target_block[None, :]).astype(jnp.float32)
        return (
            total
            + jnp.dot(
                select,
                grad_block,
                precision=lax.Precision.HIGHEST,
                preferred_element_type=jnp.float32,
            ),
            None,
        )

    dense, _ = lax.scan(
        add_source, jnp.zeros((rows_dev, col_width), jnp.float32), (got_grad, got_target)
    )
    full_width = col_width * lax.axis_size("col")
    gradient = lax.psum(dense, "dp")
    squares = lax.psum(jnp.sum(gradient * gradient, axis=1), "col")
    new_weights, new_first, new_second = adam_rows(
        placed_weights, placed_first, placed_second, gradient, squares, full_width
    )
    return (new_weights, new_first, new_second)


def solution(mesh):
    placed = (
        P("table", "col"),
        P("table", "col"),
        P("table"),
        P(),
        P(("table", "dp"), "col"),
        P(("table", "dp"), None),
        P(("table", "dp"), None, None),
        P(("table", "dp"), None),
    )
    return jax.shard_map(
        on_device,
        mesh=mesh,
        in_specs=placed,
        out_specs=(P("table", "col"), P("table", "col"), P("table")),
        check_vma=False,
    )
```

profile of v0, /device:TPU:1, one launch (start us, length us, event | category | flops | bytes accessed | tf_op | source)
XLA Modules:
  0.0 479.1 jit_solution(15004162492710192044)
XLA Ops:
  7.2 3.2 copy.52
  10.4 1.3 copy.53
  11.9 10.8 %gather_fusion = s32[4096,2]{1,0:T(8,128)S(1)} fusion(s32[16,2]{1,0:T(8,128)S(1)} %copy.21, s32[4096]{0:T(1024)S(1)} %broadcast_clamp_fusion.1), kind=kCustom, calls=%fused_computation | custom fusion | bytes 81920 | tf_op jit(solution)/shard_map/gather | solution.py:29
  22.7 14.1 %gather_fusion.1 = s32[4096,2]{1,0:T(8,128)} fusion(s32[16,2]{1,0:T(8,128)S(1)} %copy.21, s32[4096]{0:T(1024)S(1)} %broadcast_clamp_fusion), kind=kCustom, calls=%fused_computation.1 | custom fusion | bytes 81920 | tf_op jit(solution)/shard_map/gather | solution.py:31
  36.8 1.3 fusion.29
  39.8 7.6 %all-to-all-start = ((s32[16,1,256]{2,1,0:T(1,128)}), s32[16,1,256]{2,1,0:T(1,128)S(1)}, u32[]{:S(2)}, u32[]{:S(2)}) async-start(s32[16,1,256]{2,1,0:T(1,128)} %copy.23), calls=%async_computation | async-start | bytes 32768 | tf_op jit(solution)/shard_map/all_to_all | solution.py:97
  47.4 217.9 %while.22 = (s32[]{:T(128)}, f32[16,256,256]{2,1,0:T(8,128)}, s32[1024,32]{0,1:T(8,128)S(1)}, s32[16]{0:T(128)S(1)}, bf16[1024,256]{1,0:T(8,128)(2,1)S(1)}, /*index=5*/s32[]{:T(128)}, s32[1]{0:T(128)}) while((s32[]{:T(128)}, f32[16,256,256]{2,1,0:T(8,128)}, s32[1024,32]{0,1:T(8,128)S(1)}, s32[16]{0:T(128)S(1)}, ...), condition=%wide.region_2.3_spmd.clone, body=%wide.region_0.2_spmd.clone.sunk | while | flops 159121664 | bytes 1968745 | solution.py:94
  48.9 11.3 %convert_reduce_fusion.2 = bf16[256,1024]{1,0:T(8,128)(2,1)S(1)} fusion(s32[1024,32]{0,1:T(8,128)S(1)} %get-tuple-element.201, s32[256]{0:T(256)S(1)} %iota_add_fusion.2), kind=kLoop, calls=%fused_computation.4.clone.1 | loop fusion | flops 24903680 | bytes 656384 | tf_op jit(solution)/shard_map/while/body/eval_jaxpr/reduce_sum | solution.py:86
  60.2 1.0 fusion.39
  62.5 11.3 %convert_reduce_fusion.2 = bf16[256,1024]{1,0:T(8,128)(2,1)S(1)} fusion(s32[1024,32]{0,1:T(8,128)S(1)} %get-tuple-element.201, s32[256]{0:T(256)S(1)} %iota_add_fusion.2), kind=kLoop, calls=%fused_computation.4.clone.1 | loop fusion | flops 24903680 | bytes 656384 | tf_op jit(solution)/shard_map/while/body/eval_jaxpr/reduce_sum | solution.py:86
  73.8 1.0 fusion.39
  76.1 11.3 %convert_reduce_fusion.2 = bf16[256,1024]{1,0:T(8,128)(2,1)S(1)} fusion(s32[1024,32]{0,1:T(8,128)S(1)} %get-tuple-element.201, s32[256]{0:T(256)S(1)} %iota_add_fusion.2), kind=kLoop, calls=%fused_computation.4.clone.1 | loop fusion | flops 24903680 | bytes 656384 | tf_op jit(solution)/shard_map/while/body/eval_jaxpr/reduce_sum | solution.py:86
  87.4 1.0 fusion.39
  89.7 11.3 %convert_reduce_fusion.2 = bf16[256,1024]{1,0:T(8,128)(2,1)S(1)} fusion(s32[1024,32]{0,1:T(8,128)S(1)} %get-tuple-element.201, s32[256]{0:T(256)S(1)} %iota_add_fusion.2), kind=kLoop, calls=%fused_computation.4.clone.1 | loop fusion | flops 24903680 | bytes 656384 | tf_op jit(solution)/shard_map/while/body/eval_jaxpr/reduce_sum | solution.py:86
  101.0 1.0 fusion.39
  103.3 11.3 %convert_reduce_fusion.2 = bf16[256,1024]{1,0:T(8,128)(2,1)S(1)} fusion(s32[1024,32]{0,1:T(8,128)S(1)} %get-tuple-element.201, s32[256]{0:T(256)S(1)} %iota_add_fusion.2), kind=kLoop, calls=%fused_computation.4.clone.1 | loop fusion | flops 24903680 | bytes 656384 | tf_op jit(solution)/shard_map/while/body/eval_jaxpr/reduce_sum | solution.py:86
  114.6 1.0 fusion.39
  116.9 11.3 %convert_reduce_fusion.2 = bf16[256,1024]{1,0:T(8,128)(2,1)S(1)} fusion(s32[1024,32]{0,1:T(8,128)S(1)} %get-tuple-element.201, s32[256]{0:T(256)S(1)} %iota_add_fusion.2), kind=kLoop, calls=%fused_computation.4.clone.1 | loop fusion | flops 24903680 | bytes 656384 | tf_op jit(solution)/shard_map/while/body/eval_jaxpr/reduce_sum | solution.py:86
  128.2 1.0 fusion.39
  130.5 11.3 %convert_reduce_fusion.2 = bf16[256,1024]{1,0:T(8,128)(2,1)S(1)} fusion(s32[1024,32]{0,1:T(8,128)S(1)} %get-tuple-element.201, s32[256]{0:T(256)S(1)} %iota_add_fusion.2), kind=kLoop, calls=%fused_computation.4.clone.1 | loop fusion | flops 24903680 | bytes 656384 | tf_op jit(solution)/shard_map/while/body/eval_jaxpr/reduce_sum | solution.py:86
  141.8 1.0 fusion.39
  144.1 11.3 %convert_reduce_fusion.2 = bf16[256,1024]{1,0:T(8,128)(2,1)S(1)} fusion(s32[1024,32]{0,1:T(8,128)S(1)} %get-tuple-element.201, s32[256]{0:T(256)S(1)} %iota_add_fusion.2), kind=kLoop, calls=%fused_computation.4.clone.1 | loop fusion | flops 24903680 | bytes 656384 | tf_op jit(solution)/shard_map/while/body/eval_jaxpr/reduce_sum | solution.py:86
  157.7 11.3 %convert_reduce_fusion.2 = bf16[256,1024]{1,0:T(8,128)(2,1)S(1)} fusion(s32[1024,32]{0,1:T(8,128)S(1)} %get-tuple-element.201, s32[256]{0:T(256)S(1)} %iota_add_fusion.2), kind=kLoop, calls=%fused_computation.4.clone.1 | loop fusion | flops 24903680 | bytes 656384 | tf_op jit(solution)/shard_map/while/body/eval_jaxpr/reduce_sum | solution.py:86
  169.0 1.0 fusion.39
  171.3 11.3 %convert_reduce_fusion.2 = bf16[256,1024]{1,0:T(8,128)(2,1)S(1)} fusion(s32[1024,32]{0,1:T(8,128)S(1)} %get-tuple-element.201, s32[256]{0:T(256)S(1)} %iota_add_fusion.2), kind=kLoop, calls=%fused_computation.4.clone.1 | loop fusion | flops 24903680 | bytes 656384 | tf_op jit(solution)/shard_map/while/body/eval_jaxpr/reduce_sum | solution.py:86
  182.6 1.0 fusion.39
  184.9 11.3 %convert_reduce_fusion.2 = bf16[256,1024]{1,0:T(8,128)(2,1)S(1)} fusion(s32[1024,32]{0,1:T(8,128)S(1)} %get-tuple-element.201, s32[256]{0:T(256)S(1)} %iota_add_fusion.2), kind=kLoop, calls=%fused_computation.4.clone.1 | loop fusion | flops 24903680 | bytes 656384 | tf_op jit(solution)/shard_map/while/body/eval_jaxpr/reduce_sum | solution.py:86
  196.2 1.0 fusion.39
  198.5 11.3 %convert_reduce_fusion.2 = bf16[256,1024]{1,0:T(8,128)(2,1)S(1)} fusion(s32[1024,32]{0,1:T(8,128)S(1)} %get-tuple-element.201, s32[256]{0:T(256)S(1)} %iota_add_fusion.2), kind=kLoop, calls=%fused_computation.4.clone.1 | loop fusion | flops 24903680 | bytes 656384 | tf_op jit(solution)/shard_map/while/body/eval_jaxpr/reduce_sum | solution.py:86
  209.8 1.0 fusion.39
  212.1 11.3 %convert_reduce_fusion.2 = bf16[256,1024]{1,0:T(8,128)(2,1)S(1)} fusion(s32[1024,32]{0,1:T(8,128)S(1)} %get-tuple-element.201, s32[256]{0:T(256)S(1)} %iota_add_fusion.2), kind=kLoop, calls=%fused_computation.4.clone.1 | loop fusion | flops 24903680 | bytes 656384 | tf_op jit(solution)/shard_map/while/body/eval_jaxpr/reduce_sum | solution.py:86
  225.7 11.3 %convert_reduce_fusion.2 = bf16[256,1024]{1,0:T(8,128)(2,1)S(1)} fusion(s32[1024,32]{0,1:T(8,128)S(1)} %get-tuple-element.201, s32[256]{0:T(256)S(1)} %iota_add_fusion.2), kind=kLoop, calls=%fused_computation.4.clone.1 | loop fusion | flops 24903680 | bytes 656384 | tf_op jit(solution)/shard_map/while/body/eval_jaxpr/reduce_sum | solution.py:86
  237.1 1.0 fusion.39
  239.3 11.3 %convert_reduce_fusion.2 = bf16[256,1024]{1,0:T(8,128)(2,1)S(1)} fusion(s32[1024,32]{0,1:T(8,128)S(1)} %get-tuple-element.201, s32[256]{0:T(256)S(1)} %iota_add_fusion.2), kind=kLoop, calls=%fused_computation.4.clone.1 | loop fusion | flops 24903680 | bytes 656384 | tf_op jit(solution)/shard_map/while/body/eval_jaxpr/reduce_sum | solution.py:86
  252.9 11.3 %convert_reduce_fusion.2 = bf16[256,1024]{1,0:T(8,128)(2,1)S(1)} fusion(s32[1024,32]{0,1:T(8,128)S(1)} %get-tuple-element.201, s32[256]{0:T(256)S(1)} %iota_add_fusion.2), kind=kLoop, calls=%fused_computation.4.clone.1 | loop fusion | flops 24903680 | bytes 656384 | tf_op jit(solution)/shard_map/while/body/eval_jaxpr/reduce_sum | solution.py:86
  264.2 1.0 fusion.39
  265.3 6.7 %all-to-all-start.1 = ((f32[16,256,256]{2,1,0:T(8,128)}), f32[16,256,256]{2,1,0:T(8,128)}, u32[]{:S(2)}, u32[]{:S(2)}) async-start(f32[16,256,256]{2,1,0:T(8,128)} %get-tuple-element.62), calls=%async_computation.1 | async-start | bytes 8388608 | tf_op jit(solution)/shard_map/all_to_all | solution.py:96
  272.1 51.8 %all-to-all-done.1 = f32[16,256,256]{2,1,0:T(8,128)} async-done(((f32[16,256,256]{2,1,0:T(8,128)}), f32[16,256,256]{2,1,0:T(8,128)}, u32[]{:S(2)}, u32[]{:S(2)}) %all-to-all-start.1) | async-done | bytes 4194336 | tf_op jit(solution)/shard_map/all_to_all | solution.py:96
  323.9 45.4 %while.23 = (s32[]{:T(128)}, f32[2048,256]{1,0:T(8,128)S(1)}, s32[16,256]{1,0:T(8,128)S(1)}, f32[16,256,256]{2,1,0:T(8,128)}, s32[]{:T(128)}, /*index=5*/s32[]{:T(128)}) while((s32[]{:T(128)}, f32[2048,256]{1,0:T(8,128)S(1)}, s32[16,256]{1,0:T(8,128)S(1)}, f32[16,256,256]{2,1,0:T(8,128)}, s32[]{:T(128)}, /*index=5*/s32[]{:T(128)}) %tuple.62), condition=%wide.region_6.7_spmd.clone, body=%wide.region_5.6_spmd.clone.sunk | while | flops 1612185600 | bytes 4460115 | solution.py:115
  323.9 2.8 convolution_add_fusion.2
  326.7 2.8 convolution_add_fusion.2
  329.6 2.8 convolution_add_fusion.2
  332.4 2.8 convolution_add_fusion.2
  335.2 2.8 convolution_add_fusion.2
  338.1 2.8 convolution_add_fusion.2
  340.9 2.8 convolution_add_fusion.2
  343.8 2.8 convolution_add_fusion.2
  346.6 2.8 convolution_add_fusion.2
  349.4 2.8 convolution_add_fusion.2
  352.3 2.8 convolution_add_fusion.2
  355.1 2.8 convolution_add_fusion.2
  358.0 2.8 convolution_add_fusion.2
  360.8 2.8 convolution_add_fusion.2
  363.6 2.8 convolution_add_fusion.2
  366.5 2.8 convolution_add_fusion.2
  369.3 1.3 copy-done
  373.5 4.6 collective-permute-start.1
  378.2 3.0 collective-permute-start
  381.3 1.2 collective-permute-done.2
  383.9 1.0 collective-permute-done
  386.2 73.0 %all-reduce.2.cloned.1.call-done = f32[2048,256]{1,0:T(8,128)} async-done(((f32[2048,256]{1,0:T(8,128)}), f32[2048,256]{1,0:T(8,128)}) %all-reduce.2.cloned.1.call-update) | async-done | bytes 2097168 | tf_op jit(solution)/shard_map/psum | solution.py:119
  459.1 1.9 multiply_reduce_fusion
  461.1 5.8 %psum.15 = f32[2048]{0:T(1024)S(1)} all-reduce(f32[2048]{0:T(1024)S(1)} %multiply_reduce_fusion), channel_id=1, replica_groups=mesh['table'=16,'dp'=8,'col'=2] {'col'}, use_global_device_ids=true, to_apply=%region_9.10 | all-reduce | flops 2048 | bytes 16384 | tf_op jit(solution)/shard_map/psum | solution.py:120
  467.5 4.8 divide_subtract_fusion
  (104 shorter events, 19.9 us)
Async XLA Ops:
  7.2 3.2 copy-start.5
  10.4 1.3 copy-start.7
  10.4 1.3 copy-start.6
  10.4 1.4 copy-start.8
  36.8 1.6 copy-start.3
  36.8 2.3 copy-start.9
  36.8 10.6 %copy-start.1 = (bf16[1024,256]{1,0:T(8,128)(2,1)S(1)}, bf16[1024,256]{1,0:T(8,128)(2,1)}, u32[]{:S(2)}) copy-start(bf16[1024,256]{1,0:T(8,128)(2,1)} %param.16) | copy-start | bytes 1572868
  36.8 10.6 %copy-start.4 = (s32[1024,32]{0,1:T(8,128)S(1)}, s32[1024,32]{0,1:T(8,128)}, u32[]{:S(2)}) copy-start(s32[1024,32]{0,1:T(8,128)} %param.17) | copy-start | bytes 393220
  39.8 225.5 %all-to-all-start = ((s32[16,1,256]{2,1,0:T(1,128)}), s32[16,1,256]{2,1,0:T(1,128)S(1)}, u32[]{:S(2)}, u32[]{:S(2)}) async-start(s32[16,1,256]{2,1,0:T(1,128)} %copy.23), calls=%async_computation | async-start | bytes 32768 | tf_op jit(solution)/shard_map/all_to_all | solution.py:97
  265.3 58.6 %all-to-all-start.1 = ((f32[16,256,256]{2,1,0:T(8,128)}), f32[16,256,256]{2,1,0:T(8,128)}, u32[]{:S(2)}, u32[]{:S(2)}) async-start(f32[16,256,256]{2,1,0:T(8,128)} %get-tuple-element.62), calls=%async_computation.1 | async-start | bytes 8388608 | tf_op jit(solution)/shard_map/all_to_all | solution.py:96
  272.0 187.1 %all-reduce.2.cloned.1.call-start = ((), (), s32[]{:S(2)}) async-start(), calls=%async_computation.2 | async-start | bytes 4194304 | tf_op jit(solution)/shard_map/psum | solution.py:119
  369.3 1.3 copy-start
  373.5 9.1 %collective-permute-start.1 = (f32[2,64,256]{2,1,0:T(8,128)S(1)}, f32[2,64,256]{2,1,0:T(8,128)S(1)}, u32[]{:S(2)}, u32[]{:S(2)}) collective-permute-start(f32[2,64,256]{2,1,0:T(8,128)S(1)} %pad_maximum_fusion.1), channel_id=1, source_target_pairs={{0,128},{128,0},{16,144},{144,16},{32,160},{160,32},{48,176},{176,... | collective-permute-start | bytes 393224 | tf_op jit(solution)/shard_map/ppermute | solution.py:20
  378.1 4.3 collective-permute-start.2
  378.2 6.7 %collective-permute-start = (f32[2,64,256]{2,1,0:T(8,128)S(1)}, f32[2,64,256]{2,1,0:T(8,128)S(1)}, u32[]{:S(2)}, u32[]{:S(2)}) collective-permute-start(f32[2,64,256]{2,1,0:T(8,128)S(1)} %pad_maximum_fusion), channel_id=1, source_target_pairs={{0,128},{128,0},{16,144},{144,16},{32,160},{160,32},{48,176},{176,... | collective-permute-start | bytes 393224 | tf_op jit(solution)/shard_map/ppermute | solution.py:20
  386.2 81.4 %copy-start.2 = (f32[2048,256]{1,0:T(8,128)S(1)}, f32[2048,256]{1,0:T(8,128)}, u32[]{:S(2)}) copy-start(f32[2048,256]{1,0:T(8,128)} %fusion.12) | copy-start | bytes 6291460
Sparse Core Ops, SparseCore 0:
  370.8 88.3 all-reduce.1
where the time goes:
time: 480 us; the launch traced here: 479 us
  other arithmetic  191 us (40%)
  waiting for transfers between devices  127 us (26%)
  matrix products  60.9 us (13%)
  local copies, waits for them, and re-layouts  45.9 us (10%)
  starting transfers between devices  22 us (5%)
  between operations  15.5 us (3%)
  loops' own time  11.2 us (2%)
  blocking collectives  5.83 us (1%)
    reduce_sum x16, other arithmetic, owner_block(): jnp.sum((dedup_map[None, :, :] == wanted[:, None, None]).astype(jnp.float...  181 us
    psum x1, waiting for transfers between devices, on_device(): gradient = lax.psum(dense, 'dp')  73 us
    all_to_all x1, waiting for transfers between devices, on_device(): lax.all_to_all(slot_grad, 'table', split_axis=0, concat_axis=0, tiled=True)  51.8 us
    dot_general x16, matrix products, add_source(): jnp.dot(select, grad_block, precision=lax.Precision.HIGHEST, preferred_el...  44.7 us
    dot_general x16, matrix products, owner_block(): jnp.dot(tally.astype(jnp.bfloat16), upstream_grad, preferred_element_type...  16.2 us
    gather x1, local copies, waits for them, and re-layouts, local_targets(): partner_piece = jnp.sum(jnp.where(matches, hot_slices[partner], 0), axis=-1)  14.1 us
    gather x1, local copies, waits for them, and re-layouts, local_targets(): matches = hot_slices[row_owner] == row_piece[..., None]  10.8 us
    another operation x1, loops' own time, on_device(): _, slot_grad = lax.scan(owner_block, 0, jnp.arange(n_table))  10.7 us
  transfers between devices with their start and end apart: 6, of which 4 were waited for; matrix products, arithmetic and copies ran while one was open for 44% of the time, Pallas kernels for 0%

commit v1 on v0

--- a/solution.py
+++ b/solution.py
@@ -116,7 +116,9 @@
         add_source, jnp.zeros((rows_dev, col_width), jnp.float32), (got_grad, got_target)
     )
     full_width = col_width * lax.axis_size("col")
-    gradient = lax.psum(dense, "dp")
+    gradient = dense
+    for hop in (1, 2, 4):
+        gradient = gradient + lax.ppermute(gradient, "dp", [(dev, dev ^ hop) for dev in range(8)])
     squares = lax.psum(jnp.sum(gradient * gradient, axis=1), "col")
     new_weights, new_first, new_second = adam_rows(
         placed_weights, placed_first, placed_second, gradient, squares, full_width

time: 480 us -> 619 us (1.29)
  waiting for transfers between devices: 127 us -> 258 us
  starting transfers between devices: 22 us -> 36.2 us
  between operations: 15.5 us -> 2.16 us
    ppermute x0 -> x3, waiting for transfers between devices: none -> 203 us  [on_device(): lax.ppermute(gradient, 'dp', [(dev, dev ^ hop) for dev in range(8)])]
    psum x1 -> x0, waiting for transfers between devices: 73 us -> none  [on_device(): gradient = lax.psum(dense, 'dp')]
    ppermute x0 -> x3, starting transfers between devices: none -> 11.4 us  [on_device(): lax.ppermute(gradient, 'dp', [(dev, dev ^ hop) for dev in range(8)])]
  transfers between devices with their start and end apart: 6 -> 8, of which waited for: 4 -> 6; matrix products, arithmetic and copies ran while one was open for 44% -> 35% of each run, Pallas kernels for 0% -> 0%
where the time goes in v1:
time: 619 us; the launch traced here: 613 us
  waiting for transfers between devices  258 us (42%)
  other arithmetic  196 us (32%)
  matrix products  60.9 us (10%)
  local copies, waits for them, and re-layouts  45.3 us (7%)
  starting transfers between devices  36.2 us (6%)
  loops' own time  11 us (2%)
    ppermute x3, waiting for transfers between devices, on_device(): lax.ppermute(gradient, 'dp', [(dev, dev ^ hop) for dev in range(8)])  203 us
    reduce_sum x16, other arithmetic, owner_block(): jnp.sum((dedup_map[None, :, :] == wanted[:, None, None]).astype(jnp.float...  181 us
    all_to_all x1, waiting for transfers between devices, on_device(): lax.all_to_all(slot_grad, 'table', split_axis=0, concat_axis=0, tiled=True)  51.8 us
    dot_general x16, matrix products, add_source(): jnp.dot(select, grad_block, precision=lax.Precision.HIGHEST, preferred_el...  44.7 us
    dot_general x16, matrix products, owner_block(): jnp.dot(tally.astype(jnp.bfloat16), upstream_grad, preferred_element_type...  16.2 us
    gather x1, local copies, waits for them, and re-layouts, local_targets(): partner_piece = jnp.sum(jnp.where(matches, hot_slices[partner], 0), axis=-1)  14.1 us
  transfers between devices with their start and end apart: 8, of which 6 were waited for; matrix products, arithmetic and copies ran while one was open for 35% of the time, Pallas kernels for 0%

profile of v1, /device:TPU:1, one launch (start us, length us, event | category | flops | bytes accessed | tf_op | source)
XLA Modules:
  0.0 613.0 jit_solution(1509271776461202597)
XLA Ops:
  1.3 3.2 copy.51
  4.5 1.3 copy.52
  6.1 10.8 %gather_fusion = s32[4096,2]{1,0:T(8,128)S(1)} fusion(s32[16,2]{1,0:T(8,128)S(1)} %copy.21, s32[4096]{0:T(1024)S(1)} %broadcast_clamp_fusion.1), kind=kCustom, calls=%fused_computation | custom fusion | bytes 81920 | tf_op jit(solution)/shard_map/gather | solution.py:29
  16.8 14.1 %gather_fusion.1 = s32[4096,2]{1,0:T(8,128)} fusion(s32[16,2]{1,0:T(8,128)S(1)} %copy.21, s32[4096]{0:T(1024)S(1)} %broadcast_clamp_fusion), kind=kCustom, calls=%fused_computation.1 | custom fusion | bytes 81920 | tf_op jit(solution)/shard_map/gather | solution.py:31
  30.9 1.3 fusion.29
  33.9 7.6 %all-to-all-start = ((s32[16,1,256]{2,1,0:T(1,128)}), s32[16,1,256]{2,1,0:T(1,128)S(1)}, u32[]{:S(2)}, u32[]{:S(2)}) async-start(s32[16,1,256]{2,1,0:T(1,128)} %copy.23), calls=%async_computation | async-start | bytes 32768 | tf_op jit(solution)/shard_map/all_to_all | solution.py:97
  41.6 217.7 %while.22 = (s32[]{:T(128)}, f32[16,256,256]{2,1,0:T(8,128)}, s32[1024,32]{0,1:T(8,128)S(1)}, s32[16]{0:T(128)S(1)}, bf16[1024,256]{1,0:T(8,128)(2,1)S(1)}, /*index=5*/s32[]{:T(128)}, s32[1]{0:T(128)}) while((s32[]{:T(128)}, f32[16,256,256]{2,1,0:T(8,128)}, s32[1024,32]{0,1:T(8,128)S(1)}, s32[16]{0:T(128)S(1)}, ...), condition=%wide.region_2.3_spmd.clone, body=%wide.region_0.2_spmd.clone.sunk | while | flops 159121664 | bytes 1968745 | solution.py:94
  42.8 11.3 %convert_reduce_fusion.2 = bf16[256,1024]{1,0:T(8,128)(2,1)S(1)} fusion(s32[1024,32]{0,1:T(8,128)S(1)} %get-tuple-element.201, s32[256]{0:T(256)S(1)} %iota_add_fusion.2), kind=kLoop, calls=%fused_computation.4.clone.1 | loop fusion | flops 24903680 | bytes 656384 | tf_op jit(solution)/shard_map/while/body/eval_jaxpr/reduce_sum | solution.py:86
  54.2 1.0 fusion.39
  56.4 11.3 %convert_reduce_fusion.2 = bf16[256,1024]{1,0:T(8,128)(2,1)S(1)} fusion(s32[1024,32]{0,1:T(8,128)S(1)} %get-tuple-element.201, s32[256]{0:T(256)S(1)} %iota_add_fusion.2), kind=kLoop, calls=%fused_computation.4.clone.1 | loop fusion | flops 24903680 | bytes 656384 | tf_op jit(solution)/shard_map/while/body/eval_jaxpr/reduce_sum | solution.py:86
  67.8 1.0 fusion.39
  70.1 11.3 %convert_reduce_fusion.2 = bf16[256,1024]{1,0:T(8,128)(2,1)S(1)} fusion(s32[1024,32]{0,1:T(8,128)S(1)} %get-tuple-element.201, s32[256]{0:T(256)S(1)} %iota_add_fusion.2), kind=kLoop, calls=%fused_computation.4.clone.1 | loop fusion | flops 24903680 | bytes 656384 | tf_op jit(solution)/shard_map/while/body/eval_jaxpr/reduce_sum | solution.py:86
  81.4 1.0 fusion.39
  83.7 11.3 %convert_reduce_fusion.2 = bf16[256,1024]{1,0:T(8,128)(2,1)S(1)} fusion(s32[1024,32]{0,1:T(8,128)S(1)} %get-tuple-element.201, s32[256]{0:T(256)S(1)} %iota_add_fusion.2), kind=kLoop, calls=%fused_computation.4.clone.1 | loop fusion | flops 24903680 | bytes 656384 | tf_op jit(solution)/shard_map/while/body/eval_jaxpr/reduce_sum | solution.py:86
  97.3 11.3 %convert_reduce_fusion.2 = bf16[256,1024]{1,0:T(8,128)(2,1)S(1)} fusion(s32[1024,32]{0,1:T(8,128)S(1)} %get-tuple-element.201, s32[256]{0:T(256)S(1)} %iota_add_fusion.2), kind=kLoop, calls=%fused_computation.4.clone.1 | loop fusion | flops 24903680 | bytes 656384 | tf_op jit(solution)/shard_map/while/body/eval_jaxpr/reduce_sum | solution.py:86
  108.6 1.0 fusion.39
  110.9 11.3 %convert_reduce_fusion.2 = bf16[256,1024]{1,0:T(8,128)(2,1)S(1)} fusion(s32[1024,32]{0,1:T(8,128)S(1)} %get-tuple-element.201, s32[256]{0:T(256)S(1)} %iota_add_fusion.2), kind=kLoop, calls=%fused_computation.4.clone.1 | loop fusion | flops 24903680 | bytes 656384 | tf_op jit(solution)/shard_map/while/body/eval_jaxpr/reduce_sum | solution.py:86
  122.2 1.0 fusion.39
  124.5 11.3 %convert_reduce_fusion.2 = bf16[256,1024]{1,0:T(8,128)(2,1)S(1)} fusion(s32[1024,32]{0,1:T(8,128)S(1)} %get-tuple-element.201, s32[256]{0:T(256)S(1)} %iota_add_fusion.2), kind=kLoop, calls=%fused_computation.4.clone.1 | loop fusion | flops 24903680 | bytes 656384 | tf_op jit(solution)/shard_map/while/body/eval_jaxpr/reduce_sum | solution.py:86
  135.8 1.0 fusion.39
  138.1 11.3 %convert_reduce_fusion.2 = bf16[256,1024]{1,0:T(8,128)(2,1)S(1)} fusion(s32[1024,32]{0,1:T(8,128)S(1)} %get-tuple-element.201, s32[256]{0:T(256)S(1)} %iota_add_fusion.2), kind=kLoop, calls=%fused_computation.4.clone.1 | loop fusion | flops 24903680 | bytes 656384 | tf_op jit(solution)/shard_map/while/body/eval_jaxpr/reduce_sum | solution.py:86
  151.7 11.3 %convert_reduce_fusion.2 = bf16[256,1024]{1,0:T(8,128)(2,1)S(1)} fusion(s32[1024,32]{0,1:T(8,128)S(1)} %get-tuple-element.201, s32[256]{0:T(256)S(1)} %iota_add_fusion.2), kind=kLoop, calls=%fused_computation.4.clone.1 | loop fusion | flops 24903680 | bytes 656384 | tf_op jit(solution)/shard_map/while/body/eval_jaxpr/reduce_sum | solution.py:86
  165.3 11.3 %convert_reduce_fusion.2 = bf16[256,1024]{1,0:T(8,128)(2,1)S(1)} fusion(s32[1024,32]{0,1:T(8,128)S(1)} %get-tuple-element.201, s32[256]{0:T(256)S(1)} %iota_add_fusion.2), kind=kLoop, calls=%fused_computation.4.clone.1 | loop fusion | flops 24903680 | bytes 656384 | tf_op jit(solution)/shard_map/while/body/eval_jaxpr/reduce_sum | solution.py:86
  178.9 11.3 %convert_reduce_fusion.2 = bf16[256,1024]{1,0:T(8,128)(2,1)S(1)} fusion(s32[1024,32]{0,1:T(8,128)S(1)} %get-tuple-element.201, s32[256]{0:T(256)S(1)} %iota_add_fusion.2), kind=kLoop, calls=%fused_computation.4.clone.1 | loop fusion | flops 24903680 | bytes 656384 | tf_op jit(solution)/shard_map/while/body/eval_jaxpr/reduce_sum | solution.py:86
  192.5 11.3 %convert_reduce_fusion.2 = bf16[256,1024]{1,0:T(8,128)(2,1)S(1)} fusion(s32[1024,32]{0,1:T(8,128)S(1)} %get-tuple-element.201, s32[256]{0:T(256)S(1)} %iota_add_fusion.2), kind=kLoop, calls=%fused_computation.4.clone.1 | loop fusion | flops 24903680 | bytes 656384 | tf_op jit(solution)/shard_map/while/body/eval_jaxpr/reduce_sum | solution.py:86
  203.8 1.0 fusion.39
  206.1 11.3 %convert_reduce_fusion.2 = bf16[256,1024]{1,0:T(8,128)(2,1)S(1)} fusion(s32[1024,32]{0,1:T(8,128)S(1)} %get-tuple-element.201, s32[256]{0:T(256)S(1)} %iota_add_fusion.2), kind=kLoop, calls=%fused_computation.4.clone.1 | loop fusion | flops 24903680 | bytes 656384 | tf_op jit(solution)/shard_map/while/body/eval_jaxpr/reduce_sum | solution.py:86
  219.7 11.3 %convert_reduce_fusion.2 = bf16[256,1024]{1,0:T(8,128)(2,1)S(1)} fusion(s32[1024,32]{0,1:T(8,128)S(1)} %get-tuple-element.201, s32[256]{0:T(256)S(1)} %iota_add_fusion.2), kind=kLoop, calls=%fused_computation.4.clone.1 | loop fusion | flops 24903680 | bytes 656384 | tf_op jit(solution)/shard_map/while/body/eval_jaxpr/reduce_sum | solution.py:86
  233.3 11.3 %convert_reduce_fusion.2 = bf16[256,1024]{1,0:T(8,128)(2,1)S(1)} fusion(s32[1024,32]{0,1:T(8,128)S(1)} %get-tuple-element.201, s32[256]{0:T(256)S(1)} %iota_add_fusion.2), kind=kLoop, calls=%fused_computation.4.clone.1 | loop fusion | flops 24903680 | bytes 656384 | tf_op jit(solution)/shard_map/while/body/eval_jaxpr/reduce_sum | solution.py:86
  246.9 11.3 %convert_reduce_fusion.2 = bf16[256,1024]{1,0:T(8,128)(2,1)S(1)} fusion(s32[1024,32]{0,1:T(8,128)S(1)} %get-tuple-element.201, s32[256]{0:T(256)S(1)} %iota_add_fusion.2), kind=kLoop, calls=%fused_computation.4.clone.1 | loop fusion | flops 24903680 | bytes 656384 | tf_op jit(solution)/shard_map/while/body/eval_jaxpr/reduce_sum | solution.py:86
  258.2 1.0 fusion.39
  259.3 6.7 %all-to-all-start.1 = ((f32[16,256,256]{2,1,0:T(8,128)}), f32[16,256,256]{2,1,0:T(8,128)}, u32[]{:S(2)}, u32[]{:S(2)}) async-start(f32[16,256,256]{2,1,0:T(8,128)} %get-tuple-element.62), calls=%async_computation.1 | async-start | bytes 8388608 | tf_op jit(solution)/shard_map/all_to_all | solution.py:96
  266.0 51.8 %all-to-all-done.1 = f32[16,256,256]{2,1,0:T(8,128)} async-done(((f32[16,256,256]{2,1,0:T(8,128)}), f32[16,256,256]{2,1,0:T(8,128)}, u32[]{:S(2)}, u32[]{:S(2)}) %all-to-all-start.1) | async-done | bytes 4194336 | tf_op jit(solution)/shard_map/all_to_all | solution.py:96
  317.8 45.4 %while.23 = (s32[]{:T(128)}, f32[2048,256]{1,0:T(8,128)S(1)}, s32[16,256]{1,0:T(8,128)S(1)}, f32[16,256,256]{2,1,0:T(8,128)}, s32[]{:T(128)}, /*index=5*/s32[]{:T(128)}) while((s32[]{:T(128)}, f32[2048,256]{1,0:T(8,128)S(1)}, s32[16,256]{1,0:T(8,128)S(1)}, f32[16,256,256]{2,1,0:T(8,128)}, s32[]{:T(128)}, /*index=5*/s32[]{:T(128)}) %tuple.60), condition=%wide.region_6.7_spmd.clone, body=%wide.region_5.6_spmd.clone.sunk | while | flops 1612185600 | bytes 4460115 | solution.py:115
  317.8 2.8 convolution_add_fusion.2
  320.7 2.8 convolution_add_fusion.2
  323.5 2.8 convolution_add_fusion.2
  326.4 2.8 convolution_add_fusion.2
  329.2 2.8 convolution_add_fusion.2
  332.0 2.8 convolution_add_fusion.2
  334.9 2.8 convolution_add_fusion.2
  337.7 2.8 convolution_add_fusion.2
  340.6 2.8 convolution_add_fusion.2
  343.4 2.8 convolution_add_fusion.2
  346.2 2.8 convolution_add_fusion.2
  349.1 2.8 convolution_add_fusion.2
  351.9 2.8 convolution_add_fusion.2
  354.8 2.8 convolution_add_fusion.2
  357.6 2.8 convolution_add_fusion.2
  360.4 2.8 convolution_add_fusion.2
  363.2 1.7 collective-permute-start.2
  365.0 41.8 %collective-permute-done.2 = f32[2048,256]{1,0:T(8,128)S(1)} collective-permute-done((f32[2048,256]{1,0:T(8,128)S(1)}, f32[2048,256]{1,0:T(8,128)S(1)}, u32[]{:S(2)}, u32[]{:S(2)}) %collective-permute-start.2) | collective-permute-done | bytes 2097184 | tf_op jit(solution)/shard_map/ppermute | solution.py:121
  406.7 1.6 add.174
  408.3 3.0 collective-permute-start.3
  411.3 90.2 %collective-permute-done.3 = f32[2048,256]{1,0:T(8,128)} collective-permute-done((f32[2048,256]{1,0:T(8,128)}, f32[2048,256]{1,0:T(8,128)}, u32[]{:S(2)}, u32[]{:S(2)}) %collective-permute-start.3) | collective-permute-done | bytes 2097184 | tf_op jit(solution)/shard_map/ppermute | solution.py:121
  501.5 2.5 add.175
  504.0 6.7 %collective-permute-start.4 = (f32[2048,256]{1,0:T(8,128)S(1)}, f32[2048,256]{1,0:T(8,128)}, u32[]{:S(2)}, u32[]{:S(2)}) collective-permute-start(f32[2048,256]{1,0:T(8,128)S(1)} %add.175), channel_id=1, source_target_pairs={{0,8},{2,10},{4,12},{6,14},{8,0},{10,2},{12,4},{14,6},{1,9},{3,11}... | collective-permute-start | bytes 6291464 | tf_op jit(solution)/shard_map/ppermute | solution.py:121
  512.7 7.4 %collective-permute-start.5 = (f32[2,64]{1,0:T(2,128)S(1)}, f32[2,64]{1,0:T(2,128)S(1)}, u32[]{:S(2)}, u32[]{:S(2)}) collective-permute-start(f32[2,64]{1,0:T(2,128)S(1)} %pad_maximum_fusion.2), channel_id=1, source_target_pairs={{0,128},{128,0},{16,144},{144,16},{32,160},{160,32},{48,176},{176,... | collective-permute-start | bytes 1544 | tf_op jit(solution)/shard_map/ppermute | solution.py:20
  521.2 3.0 collective-permute-start
  524.4 2.5 collective-permute-done.1
  530.3 70.9 %collective-permute-done.4 = f32[2048,256]{1,0:T(8,128)} collective-permute-done((f32[2048,256]{1,0:T(8,128)S(1)}, f32[2048,256]{1,0:T(8,128)}, u32[]{:S(2)}, u32[]{:S(2)}) %collective-permute-start.4) | collective-permute-done | bytes 2097184 | tf_op jit(solution)/shard_map/ppermute | solution.py:121
  601.2 1.9 multiply_reduce_fusion
  603.2 3.8 psum.7
  607.6 5.5 divide_subtract_fusion
  (103 shorter events, 26.5 us)
Async XLA Ops:
  1.3 3.2 copy-start.3
  4.5 1.3 copy-start.4
  4.5 1.4 copy-start.5
  30.9 1.6 copy-start.1
  30.9 2.3 copy-start.6
  30.9 10.6 %copy-start = (bf16[1024,256]{1,0:T(8,128)(2,1)S(1)}, bf16[1024,256]{1,0:T(8,128)(2,1)}, u32[]{:S(2)}) copy-start(bf16[1024,256]{1,0:T(8,128)(2,1)} %param.16) | copy-start | bytes 1572868
  30.9 10.6 %copy-start.2 = (s32[1024,32]{0,1:T(8,128)S(1)}, s32[1024,32]{0,1:T(8,128)}, u32[]{:S(2)}) copy-start(s32[1024,32]{0,1:T(8,128)} %param.17) | copy-start | bytes 393220
  33.9 225.3 %all-to-all-start = ((s32[16,1,256]{2,1,0:T(1,128)}), s32[16,1,256]{2,1,0:T(1,128)S(1)}, u32[]{:S(2)}, u32[]{:S(2)}) async-start(s32[16,1,256]{2,1,0:T(1,128)} %copy.23), calls=%async_computation | async-start | bytes 32768 | tf_op jit(solution)/shard_map/all_to_all | solution.py:97
  259.3 58.6 %all-to-all-start.1 = ((f32[16,256,256]{2,1,0:T(8,128)}), f32[16,256,256]{2,1,0:T(8,128)}, u32[]{:S(2)}, u32[]{:S(2)}) async-start(f32[16,256,256]{2,1,0:T(8,128)} %get-tuple-element.62), calls=%async_computation.1 | async-start | bytes 8388608 | tf_op jit(solution)/shard_map/all_to_all | solution.py:96
  363.2 43.5 %collective-permute-start.2 = (f32[2048,256]{1,0:T(8,128)S(1)}, f32[2048,256]{1,0:T(8,128)S(1)}, u32[]{:S(2)}, u32[]{:S(2)}) collective-permute-start(f32[2048,256]{1,0:T(8,128)S(1)} %get-tuple-element.63), channel_id=1, source_target_pairs={{0,2},{2,0},{4,6},{6,4},{8,10},{10,8},{12,14},{14,12},{1,3},{3,1},... | collective-permute-start | bytes 6291464 | tf_op jit(solution)/shard_map/ppermute | solution.py:121
  408.3 93.2 %collective-permute-start.3 = (f32[2048,256]{1,0:T(8,128)}, f32[2048,256]{1,0:T(8,128)}, u32[]{:S(2)}, u32[]{:S(2)}) collective-permute-start(f32[2048,256]{1,0:T(8,128)} %add.174), channel_id=1, source_target_pairs={{0,4},{2,6},{4,0},{6,2},{8,12},{10,14},{12,8},{14,10},{1,5},{3,7},... | collective-permute-start | bytes 6291464 | tf_op jit(solution)/shard_map/ppermute | solution.py:121
  504.0 97.2 %collective-permute-start.4 = (f32[2048,256]{1,0:T(8,128)S(1)}, f32[2048,256]{1,0:T(8,128)}, u32[]{:S(2)}, u32[]{:S(2)}) collective-permute-start(f32[2048,256]{1,0:T(8,128)S(1)} %add.175), channel_id=1, source_target_pairs={{0,8},{2,10},{4,12},{6,14},{8,0},{10,2},{12,4},{14,6},{1,9},{3,11}... | collective-permute-start | bytes 6291464 | tf_op jit(solution)/shard_map/ppermute | solution.py:121
  512.7 11.5 %collective-permute-start.5 = (f32[2,64]{1,0:T(2,128)S(1)}, f32[2,64]{1,0:T(2,128)S(1)}, u32[]{:S(2)}, u32[]{:S(2)}) collective-permute-start(f32[2,64]{1,0:T(2,128)S(1)} %pad_maximum_fusion.2), channel_id=1, source_target_pairs={{0,128},{128,0},{16,144},{144,16},{32,160},{160,32},{48,176},{176,... | collective-permute-start | bytes 1544 | tf_op jit(solution)/shard_map/ppermute | solution.py:20
  521.1 5.8 collective-permute-start.1
  521.2 7.8 %collective-permute-start = (f32[2,64,256]{2,1,0:T(8,128)S(1)}, f32[2,64,256]{2,1,0:T(8,128)S(1)}, u32[]{:S(2)}, u32[]{:S(2)}) collective-permute-start(f32[2,64,256]{2,1,0:T(8,128)S(1)} %pad_maximum_fusion), channel_id=1, source_target_pairs={{0,128},{128,0},{16,144},{144,16},{32,160},{160,32},{48,176},{176,... | collective-permute-start | bytes 393224 | tf_op jit(solution)/shard_map/ppermute | solution.py:20
